TPU v7x, 256 devices: a whole 4x4x8 slice. The times are simulated.
256 devices in a mesh: line: 4 (over y), patch: 64 (over x, z, core).
Axes of the slice: x: 4, y: 4, z: 8, core: 2. Of those that a mesh axis runs over, the one named last changes fastest.
Arguments:
- newton_residual: float32 [8, 48, 64, 128], P('line', None, 'patch'), may hold values from -24 to 24
- diag_block: bfloat16 [8, 48, 48, 64, 128], P('line', None, None, 'patch'), may hold values from -0.6 to 5
- lower: bfloat16 [8, 48, 48, 64, 128], P('line', None, None, 'patch'), may hold values from -1.296875 to 1.296875
- upper: bfloat16 [8, 48, 48, 64, 128], P('line', None, None, 'patch'), may hold values from -1.296875 to 1.296875
- west: bfloat16 [8, 48, 48, 64, 128], P('line', None, None, 'patch'), may hold values from -0.5390625 to 0.5390625
- east: bfloat16 [8, 48, 48, 64, 128], P('line', None, None, 'patch'), may hold values from -0.5390625 to 0.5390625
- pivot_inverse: bfloat16 [8, 48, 48, 64, 128], P('line', None, None, 'patch'), may hold values from -0.05 to 0.34
Outputs:
- newton_step: float32 [8, 48, 64, 128], P('line', None, 'patch')
All inputs are finite; a program needn't handle non-finite values.
Results may differ from a plain program's by a relative error of at most 0.0003.
Values sent between devices are 32-bit elements; how exact they have to be, the bound alone decides.
A program may use at most 64 MiB of HBM per device.

v0:
```python
import functools

import jax
import jax.numpy as jnp
from jax import lax
from jax.experimental import pallas as pl
from jax.experimental.pallas import tpu as pltpu
from jax.sharding import PartitionSpec as P

MESH = pl.DeviceIdType.MESH
F32 = jnp.float32
B = 48
N = 4
SCALE = 2.0**-15
PIV, LOW, UP, DIAG, WEST, EAST = range(6)
GROUP = 16


def kernel(
    lines, rows,
    r_hbm, piv_hbm, low_hbm, up_hbm, diag_hbm, west_hbm, east_hbm,
    out_ref,
    packed, mats, xin, u, d, z, g, gin, zin, zlow, hw, he, bacc, tmp,
    part1, recv1, part2, recv2, res, gam, coef, eta,
    load_sem, carry_send, carry_recv, up_send, up_recv, low_send, low_recv,
    west_send, west_recv, east_send, east_recv, red1_send, red1_recv, red2_send, red2_recv,
):
    y = lax.axis_index("line")
    p = lax.axis_index("patch")
    hbm = (piv_hbm, low_hbm, up_hbm, diag_hbm, west_hbm, east_hbm)

    def load(a, k):
        return pltpu.make_async_copy(hbm[a].at[k], packed.at[a, k], load_sem.at[a, k])

    load_r = pltpu.make_async_copy(r_hbm, tmp, load_sem.at[6, 0])
    load_r.start()
    for a in range(6):
        for k in range(2):
            load(a, k).start()

    x, b = p // GROUP, p % GROUP
    a_me = y * 4 + x

    def peer1(o):
        i = lax.rem(a_me + o, GROUP)
        return (i // 4, (i % 4) * GROUP + b)

    def peer2(o):
        return (y, x * GROUP + lax.rem(b + o, GROUP))

    has_down, has_up = y > 0, y < lines - 1
    has_west, has_east = p > 0, p < rows - 1

    barrier = pltpu.get_barrier_semaphore()
    for o in range(1, GROUP):
        pl.semaphore_signal(barrier, inc=1, device_id=peer1(o), device_id_type=MESH)
        pl.semaphore_signal(barrier, inc=1, device_id=peer2(o), device_id_type=MESH)

    @pl.when(has_west)
    def _():
        pl.semaphore_signal(barrier, inc=1, device_id=(y, p - 1), device_id_type=MESH)

    @pl.when(has_east)
    def _():
        pl.semaphore_signal(barrier, inc=1, device_id=(y, p + 1), device_id_type=MESH)

    u[...] = jnp.zeros_like(u)
    d[...] = jnp.zeros_like(d)
    xin[1:] = jnp.zeros_like(xin[1:])
    part1[...] = jnp.zeros_like(part1)
    coef[...] = jnp.zeros_like(coef)
    eta[...] = jnp.ones_like(eta)
    gam[...] = jnp.ones_like(gam)

    @pl.when(jnp.logical_not(has_west))
    def _():
        hw[...] = jnp.zeros_like(hw)

    @pl.when(jnp.logical_not(has_east))
    def _():
        he[...] = jnp.zeros_like(he)

    @pl.when(jnp.logical_not(has_down))
    def _():
        zlow[...] = jnp.zeros_like(zlow)

    load_r.wait()
    xin[0] = tmp[...] * SCALE

    def widen(a, k):
        def body(t, carry):
            for s in range(4):
                i = t * 4 + s
                mats[a, k, pl.ds(i, B, stride=B), :] = packed[a, k, i].astype(F32)
            return carry
        lax.fori_loop(0, B // 4, body, 0)

    def widen_all(first, last):
        for a in range(first, last):
            for k in range(2):
                load(a, k).wait()
        def body(t, carry):
            widen(t // 2, t % 2)
            return carry
        lax.fori_loop(2 * first, 2 * last, body, 0)

    def apply(pairs, start=None):
        step = 8
        def body(t, accs):
            accs = list(accs)
            for s in range(step):
                j = t * step + s
                for a, k, v in pairs:
                    row = v[pl.ds(j, 8, stride=0), :]
                    block = mats[a, k, pl.ds(pl.multiple_of(j * B, 8), B), :].reshape(6, 8, 128)
                    accs[s % 2] = accs[s % 2] + block * row[None]
            return tuple(accs)
        zero = jnp.zeros((6, 8, 128), F32)
        one = zero if start is None else start.reshape(6, 8, 128)
        one, two = lax.fori_loop(0, B // step, body, (one, zero))
        return (one + two).reshape(B, 128)

    def send(src, dst, ssem, rsem, to):
        return pltpu.make_async_remote_copy(
            src_ref=src, dst_ref=dst, send_sem=ssem, recv_sem=rsem, device_id=to, device_id_type=MESH
        )

    def send_carry(n):
        return send(g.at[n, 1], gin.at[n], carry_send.at[n], carry_recv.at[n], (y + 1, p))

    def send_up(n):
        return send(z.at[n, 0], zin.at[n], up_send.at[n], up_recv.at[n], (y - 1, p))

    def send_low(n):
        return send(z.at[n, 1], zlow.at[n], low_send.at[n], low_recv.at[n], (y + 1, p))

    def send_west(n, k):
        return send(z.at[n, k], he.at[n, k], west_send.at[n, k], west_recv.at[n, k], (y, p - 1))

    def send_east(n, k):
        return send(z.at[n, k], hw.at[n, k], east_send.at[n, k], east_recv.at[n, k], (y, p + 1))

    def down_rest(n):
        tmp[0] = xin[n, 1] - apply([(LOW, 1, g.at[n, 0])])
        g[n, 1] = apply([(PIV, 1, tmp.at[0])])

    def red_start(m):
        q0, q1 = xin[m + 1, 0].reshape(6, 8, 128), xin[m + 1, 1].reshape(6, 8, 128)

        def row(i, a0, a1, b0, b1):
            s = jnp.sum(a0 * b0 + a1 * b1, axis=0)
            part1[m, pl.ds(i, 1), :] = jnp.sum(s, axis=0, keepdims=True)

        for i in range(N):
            row(i, u[i, 0].reshape(6, 8, 128), u[i, 1].reshape(6, 8, 128), q0, q1)
        v0, v1 = u[m, 0].reshape(6, 8, 128), u[m, 1].reshape(6, 8, 128)
        row(4, v0, v1, v0, v1)
        row(5, q0, q1, q0, q1)
        for o in range(1, GROUP):
            send(part1.at[m], recv1.at[m, o - 1], red1_send.at[m], red1_recv.at[m], peer1(o)).start()

    def red_middle(m):
        pltpu.make_async_copy(recv1.at[m], recv1.at[m], red1_recv.at[m]).wait()
        part2[m] = part1[m] + jnp.sum(recv1[m], axis=0)
        for o in range(1, GROUP):
            send(part2.at[m], recv2.at[m, o - 1], red2_send.at[m], red2_recv.at[m], peer2(o)).start()

    def red_end(m):
        pltpu.make_async_copy(recv2.at[m], recv2.at[m], red2_recv.at[m]).wait()
        total = part2[m] + jnp.sum(recv2[m], axis=0)
        res[m] = jnp.broadcast_to(jnp.sum(total, axis=1, keepdims=True), (8, 128))
        gam[m] = res[m, pl.ds(4, 8, stride=0), :]
        for i in range(N):
            value = res[m, pl.ds(i, 8, stride=0), :] / gam[i]
            coef[i] = jnp.where(m >= i, value, 0.0)
        eta[...] = 1.0 / jnp.sqrt(res[m, pl.ds(5, 8, stride=0), :])

    def combined(value, olds):
        total = value.reshape(6, 8, 128)
        for i in range(N):
            total = total - coef[i][None] * olds(i).reshape(6, 8, 128)
        return (total * eta[...][None]).reshape(B, 128)

    widen_all(0, 2)

    @pl.when(has_down)
    def _():
        widen_all(2, 6)

    first = True

    def stage(n, carry):
        @pl.when(jnp.logical_not(has_down))
        def _():
            g[n, 0] = apply([(PIV, 0, xin.at[n, 0])])
            down_rest(n)

        @pl.when(n == 0)
        def _():
            pl.semaphore_wait(barrier, 2 * (GROUP - 1) + has_west.astype(jnp.int32) + has_east.astype(jnp.int32))

        @pl.when(jnp.logical_not(has_down))
        def _():
            send_carry(n).start()

            @pl.when(n == 0)
            def _():
                widen_all(2, 6)

        @pl.when(n > 0)
        def _():
            red_start(n - 1)

        @pl.when(has_down)
        def _():
            send_carry(n).wait_recv()
            tmp[1] = xin[n, 0] - apply([(LOW, 0, gin.at[n])])
            g[n, 0] = apply([(PIV, 0, tmp.at[1])])
            down_rest(n)

            @pl.when(has_up)
            def _():
                send_carry(n).start()

        @pl.when(jnp.logical_and(n > 0, has_up))
        def _():
            red_middle(n - 1)

        @pl.when(has_up)
        def _():
            send_up(n).wait_recv()
            bacc[1] = apply([(UP, 1, zin.at[n])])
            z[n, 1] = g[n, 1] - apply([(PIV, 1, bacc.at[1])])
            send_low(n).start()

        @pl.when(jnp.logical_not(has_up))
        def _():
            bacc[1] = jnp.zeros((B, 128), F32)
            z[n, 1] = g[n, 1]

        @pl.when(has_west)
        def _():
            send_west(n, 1).start()

        @pl.when(has_east)
        def _():
            send_east(n, 1).start()

        bacc[0] = apply([(UP, 0, z.at[n, 1])])
        z[n, 0] = g[n, 0] - apply([(PIV, 0, bacc.at[0])])

        @pl.when(has_down)
        def _():
            send_up(n).start()

        @pl.when(has_west)
        def _():
            send_west(n, 0).start()

        @pl.when(has_east)
        def _():
            send_east(n, 0).start()

        @pl.when(jnp.logical_and(n > 0, jnp.logical_not(has_up)))
        def _():
            red_middle(n - 1)

        bacc[1] = apply([(DIAG, 1, z.at[n, 1]), (LOW, 1, z.at[n, 0])], bacc[1])
        bacc[0] = apply([(DIAG, 0, z.at[n, 0])], bacc[0])

        @pl.when(n > 0)
        def _():
            red_end(n - 1)

        for k in range(2):
            u[n, k] = combined(xin[n, k], lambda i: u[i, k])
            d[n, k] = combined(z[n, k], lambda i: d[i, k])

        def halo(k):
            @pl.when(has_west)
            def _():
                send_east(n, k).wait_recv()

            @pl.when(has_east)
            def _():
                send_west(n, k).wait_recv()

        halo(1)
        value = apply([(WEST, 1, hw.at[n, 1]), (EAST, 1, he.at[n, 1])], bacc[1])
        xin[n + 1, 1] = combined(value, lambda i: xin[i + 1, 1])

        @pl.when(has_down)
        def _():
            send_low(n).wait_recv()
            bacc[0] = apply([(LOW, 0, zlow.at[n])], bacc[0])

        halo(0)
        value = apply([(WEST, 0, hw.at[n, 0]), (EAST, 0, he.at[n, 0])], bacc[0])
        xin[n + 1, 0] = combined(value, lambda i: xin[i + 1, 0])
        return carry

    lax.fori_loop(0, N, stage, 0)
    red_start(N - 1)
    red_middle(N - 1)
    red_end(N - 1)

    size = [jnp.sqrt(gam[i]) for i in range(N)]
    zero = jnp.zeros((8, 128), F32)

    def entry(m, i):
        return res[m, pl.ds(i, 8, stride=0), :]

    hess = [[zero] * N for _ in range(N + 1)]
    for m in range(N):
        for i in range(m + 1):
            hess[i][m] = entry(m, i) / (size[i] * size[m])
        if m < N - 1:
            hess[m + 1][m] = size[m + 1] * jnp.sqrt(entry(m, 5)) / size[m]
        else:
            rest = entry(m, 5)
            for i in range(N):
                rest = rest - entry(m, i) * entry(m, i) / gam[i]
            hess[N][m] = jnp.sqrt(jnp.maximum(rest, 0.0)) / size[m]
    target = [size[0]] + [zero] * N
    for j in range(N):
        one, two = hess[j][j], hess[j + 1][j]
        radius = jnp.sqrt(one * one + two * two)
        cosine, sine = one / radius, two / radius
        top = [cosine * hess[j][i] + sine * hess[j + 1][i] for i in range(N)]
        hess[j + 1] = [cosine * hess[j + 1][i] - sine * hess[j][i] for i in range(N)]
        hess[j] = top
        target[j], target[j + 1] = (
            cosine * target[j] + sine * target[j + 1],
            cosine * target[j + 1] - sine * target[j],
        )
    answer = [None] * N
    for i in reversed(range(N)):
        value = target[i]
        for k in range(i + 1, N):
            value = value - hess[i][k] * answer[k]
        answer[i] = value / hess[i][i]
    for k in range(2):
        total = jnp.zeros((6, 8, 128), F32)
        for i in range(N):
            total = total + (answer[i] / size[i])[None] * d[i, k].reshape(6, 8, 128)
        out_ref[k] = total.reshape(B, 128)

    def drain(n, carry):
        @pl.when(has_up)
        def _():
            send_carry(n).wait_send()
            send_low(n).wait_send()

        @pl.when(has_down)
        def _():
            send_up(n).wait_send()

        for k in range(2):
            @pl.when(has_west)
            def _():
                send_west(n, k).wait_send()

            @pl.when(has_east)
            def _():
                send_east(n, k).wait_send()

        pltpu.make_async_copy(recv1.at[n], recv1.at[n], red1_send.at[n]).wait()
        pltpu.make_async_copy(recv2.at[n], recv2.at[n], red2_send.at[n]).wait()
        return carry

    lax.fori_loop(0, N, drain, 0)


def solution(mesh):
    lines, rows = mesh.shape["line"], mesh.shape["patch"]
    dma = pltpu.SemaphoreType.DMA
    pair = pltpu.VMEM((N, 2, B, 128), F32)
    single = pltpu.VMEM((N, B, 128), F32)
    tile = pltpu.VMEM((N, 8, 128), F32)
    tiles = pltpu.VMEM((N, GROUP - 1, 8, 128), F32)

    def per_device(newton_residual, diag_block, lower, upper, west, east, pivot_inverse):
        arrays = [a.reshape(2, B, B, 128) for a in (pivot_inverse, lower, upper, diag_block, west, east)]
        step = pl.pallas_call(
            functools.partial(kernel, lines, rows),
            out_shape=jax.ShapeDtypeStruct((2, B, 128), F32),
            in_specs=[pl.BlockSpec(memory_space=pl.ANY)] * 7,
            out_specs=pl.BlockSpec(memory_space=pltpu.VMEM),
            scratch_shapes=[
                pltpu.VMEM((6, 2, B, B, 128), jnp.bfloat16),
                pltpu.VMEM((6, 2, B * B, 128), F32),
                pltpu.VMEM((N + 1, 2, B, 128), F32),
                pair, pair, pair, pair,
                single, single, single,
                pair, pair,
                pltpu.VMEM((2, B, 128), F32), pltpu.VMEM((2, B, 128), F32),
                tile, tiles, tile, tiles, tile,
                tile, tile,
                pltpu.VMEM((8, 128), F32),
                dma((7, 2)),
                dma((N,)), dma((N,)), dma((N,)), dma((N,)), dma((N,)), dma((N,)),
                dma((N, 2)), dma((N, 2)), dma((N, 2)), dma((N, 2)),
                dma((N,)), dma((N,)), dma((N,)), dma((N,)),
            ],
            compiler_params=pltpu.CompilerParams(collective_id=0, has_side_effects=True),
        )(newton_residual.reshape(2, B, 128), *arrays)
        return (step * (1.0 / SCALE)).reshape(2, B, 1, 128)

    mats = P("line", None, None, "patch", None)
    return jax.shard_map(
        per_device,
        mesh=mesh,
        in_specs=(P("line", None, "patch", None), mats, mats, mats, mats, mats, mats),
        out_specs=P("line", None, "patch", None),
        check_vma=False,
    )
```

profile of v0, /device:TPU:1, one launch (start us, length us, event | category | flops | bytes accessed | tf_op | source)
XLA Modules:
  0.0 112.2 jit_solution(10667299459564829945)
XLA Ops:
  0.0 110.7 %shard_map.73 = f32[2,48,128]{2,1,0:T(8,128)} custom-call(f32[2,48,128]{2,1,0:T(8,128)} %bitcast.16, bf16[2,48,48,128]{3,2,1,0:T(8,128)(2,1)} %bitcast.10, bf16[2,48,48,128]{3,2,1,0:T(8,128)(2,1)} %bitcast.11, bf16[2,48,48,128]{3,2,1,0:T(8,128)(2,1)} %bitcast.12, bf16[2,48,48,128]{3,2,1,0:T(8,128)(2,1)} %bitcast.13, bf16[2,48,48,128]{3,2,1,0:T(8,128)(2,1)} %bitcast.14, ...), custom_call_target="tpu_custom_call" | custom-call | tf_op jit(solution)/shard_map/pallas_call | solution.py:384
  110.7 1.4 %broadcast_multiply_fusion = f32[2,48,128]{2,1,0:T(8,128)} fusion(f32[2,48,128]{2,1,0:T(8,128)} %shard_map.73), kind=kLoop, calls=%fused_computation | loop fusion | flops 12288 | bytes 98304 | tf_op jit(solution)/shard_map/mul | solution.py:407
where the time goes:
time: 112 us
  Pallas kernels  111 us (99%)
  other arithmetic  1.42 us (1%)
    pallas_call x1, Pallas kernels, per_device(): pl.pallas_call(functools.partial(kernel, lines, rows), out_shape=jax.Shap...  111 us

commit v1 on v0

--- a/solution.py
+++ b/solution.py
@@ -14,6 +14,7 @@
 SCALE = 2.0**-15
 PIV, LOW, UP, DIAG, WEST, EAST = range(6)
 GROUP = 16
+PITCH = 56
 
 
 def kernel(
@@ -21,9 +22,10 @@
     r_hbm, piv_hbm, low_hbm, up_hbm, diag_hbm, west_hbm, east_hbm,
     out_ref,
     packed, mats, xin, u, d, z, g, gin, zin, zlow, hw, he, bacc, tmp,
-    part1, recv1, part2, recv2, res, gam, coef, eta,
+    part1, recv1, part2, recv2, res, gam, coef, eta, over, held, far, mine, loc, col, gsum,
     load_sem, carry_send, carry_recv, up_send, up_recv, low_send, low_recv,
     west_send, west_recv, east_send, east_recv, red1_send, red1_recv, red2_send, red2_recv,
+    over_send, over_recv, far_send, far_recv,
 ):
     y = lax.axis_index("line")
     p = lax.axis_index("patch")
@@ -34,9 +36,8 @@
 
     load_r = pltpu.make_async_copy(r_hbm, tmp, load_sem.at[6, 0])
     load_r.start()
-    for a in range(6):
-        for k in range(2):
-            load(a, k).start()
+    for a, k in ((PIV, 0), (PIV, 1), (LOW, 1), (LOW, 0), (UP, 1), (UP, 0), (DIAG, 0), (DIAG, 1), (WEST, 1), (EAST, 1), (WEST, 0), (EAST, 0)):
+        load(a, k).start()
 
     x, b = p // GROUP, p % GROUP
     a_me = y * 4 + x
@@ -88,37 +89,34 @@
     xin[0] = tmp[...] * SCALE
 
     def widen(a, k):
+        pltpu.make_async_copy(packed.at[a, k], packed.at[a, k], load_sem.at[a, k]).wait()
+
         def body(t, carry):
-            for s in range(4):
-                i = t * 4 + s
-                mats[a, k, pl.ds(i, B, stride=B), :] = packed[a, k, i].astype(F32)
+            for s in range(8):
+                i = t * 8 + s
+                mats[a, k, pl.ds(i, B, stride=PITCH), :] = packed[a, k, i].astype(F32)
             return carry
-        lax.fori_loop(0, B // 4, body, 0)
+        lax.fori_loop(0, B // 8, body, 0)
 
     def widen_all(first, last):
-        for a in range(first, last):
-            for k in range(2):
-                load(a, k).wait()
         def body(t, carry):
             widen(t // 2, t % 2)
             return carry
-        lax.fori_loop(2 * first, 2 * last, body, 0)
+        lax.fori_loop(first, last, body, 0)
+
+    def block(a, k):
+        return mats.at[a, k], PITCH
 
     def apply(pairs, start=None):
-        step = 8
-        def body(t, accs):
-            accs = list(accs)
-            for s in range(step):
-                j = t * step + s
-                for a, k, v in pairs:
-                    row = v[pl.ds(j, 8, stride=0), :]
-                    block = mats[a, k, pl.ds(pl.multiple_of(j * B, 8), B), :].reshape(6, 8, 128)
-                    accs[s % 2] = accs[s % 2] + block * row[None]
-            return tuple(accs)
         zero = jnp.zeros((6, 8, 128), F32)
-        one = zero if start is None else start.reshape(6, 8, 128)
-        one, two = lax.fori_loop(0, B // step, body, (one, zero))
-        return (one + two).reshape(B, 128)
+        accs = [zero if start is None else start.reshape(6, 8, 128), zero]
+        turn = 0
+        for (columns, pitch), v in pairs:
+            for j in range(B):
+                row = v[pl.ds(j, 8, stride=0), :]
+                accs[turn] = accs[turn] + columns[pl.ds(j * pitch, B), :].reshape(6, 8, 128) * row[None]
+                turn = 1 - turn
+        return (accs[0] + accs[1]).reshape(B, 128)
 
     def send(src, dst, ssem, rsem, to):
         return pltpu.make_async_remote_copy(
@@ -140,9 +138,26 @@
     def send_east(n, k):
         return send(z.at[n, k], hw.at[n, k], east_send.at[n, k], east_recv.at[n, k], (y, p + 1))
 
-    def down_rest(n):
-        tmp[0] = xin[n, 1] - apply([(LOW, 1, g.at[n, 0])])
-        g[n, 1] = apply([(PIV, 1, tmp.at[0])])
+    def send_far(n):
+        return send(mine.at[n], far.at[n], far_send.at[n], far_recv.at[n], (jnp.where(y == 0, y + 2, y - 2), p))
+
+    order = jnp.where(y == 1, 0, 1)
+    coupling = jnp.where(y == 1, LOW, UP)
+
+    def form(first, last):
+        def body(j, carry):
+            a = apply([((mats.at[PIV, order], PITCH), mats.at[coupling, order, pl.ds(pl.multiple_of(j * PITCH, 8), B)])])
+            col[0] = a
+            col[1] = apply([((mats.at[coupling, 1 - order], PITCH), col.at[0])])
+            over[pl.ds(pl.multiple_of(j * B, 8), B), :] = apply([((mats.at[PIV, 1 - order], PITCH), col.at[1])])
+            rows_j = pl.ds(pl.multiple_of(j * B, 8), B)
+            send(over.at[rows_j], held.at[rows_j], over_send, over_recv, (jnp.where(y == 1, y - 1, y + 1), p)).start()
+            return carry
+        lax.fori_loop(first, last, body, 0)
+
+    def down_rest(n, dst):
+        tmp[0] = xin[n, 1] - apply([(block(LOW, 1), dst.at[n, 0])])
+        dst[n, 1] = apply([(block(PIV, 1), tmp.at[0])])
 
     def red_start(m):
         q0, q1 = xin[m + 1, 0].reshape(6, 8, 128), xin[m + 1, 1].reshape(6, 8, 128)
@@ -181,56 +196,115 @@
             total = total - coef[i][None] * olds(i).reshape(6, 8, 128)
         return (total * eta[...][None]).reshape(B, 128)
 
+    inner = jnp.logical_or(y == 1, y == 2)
+    outer = jnp.logical_not(inner)
+
     widen_all(0, 2)
+    widen(LOW, 1)
 
     @pl.when(has_down)
     def _():
-        widen_all(2, 6)
-
-    first = True
+        widen(LOW, 0)
+        widen_all(4, 12)
 
     def stage(n, carry):
-        @pl.when(jnp.logical_not(has_down))
-        def _():
-            g[n, 0] = apply([(PIV, 0, xin.at[n, 0])])
-            down_rest(n)
+        later = n > 0
+
+        @pl.when(y == 0)
+        def _():
+            g[n, 0] = apply([(block(PIV, 0), xin.at[n, 0])])
+            down_rest(n, g)
 
         @pl.when(n == 0)
         def _():
             pl.semaphore_wait(barrier, 2 * (GROUP - 1) + has_west.astype(jnp.int32) + has_east.astype(jnp.int32))
 
-        @pl.when(jnp.logical_not(has_down))
+        @pl.when(jnp.logical_and(y == 0, later))
+        def _():
+            @pl.when(n == 1)
+            def _():
+                pltpu.make_async_copy(held, held, over_recv).wait()
+
+            mine[n] = apply([((held, B), g.at[n, 1])])
+            send_far(n).start()
+
+        @pl.when(y == 0)
         def _():
             send_carry(n).start()
 
             @pl.when(n == 0)
             def _():
-                widen_all(2, 6)
-
-        @pl.when(n > 0)
+                widen(LOW, 0)
+                widen_all(4, 12)
+
+        @pl.when(jnp.logical_and(y == 1, later))
+        def _():
+            loc[n, 0] = apply([(block(PIV, 0), xin.at[n, 0])])
+            down_rest(n, loc)
+            send(loc.at[n, 1], gin.at[n], carry_send.at[n], carry_recv.at[n], (y + 1, p)).start()
+
+        @pl.when(later)
         def _():
             red_start(n - 1)
 
+        @pl.when(jnp.logical_and(y == 3, later))
+        def _():
+            red_middle(n - 1)
+
+        @pl.when(jnp.logical_and(y == 2, n == 0))
+        def _():
+            form(0, 8)
+
         @pl.when(has_down)
         def _():
             send_carry(n).wait_recv()
-            tmp[1] = xin[n, 0] - apply([(LOW, 0, gin.at[n])])
-            g[n, 0] = apply([(PIV, 0, tmp.at[1])])
-            down_rest(n)
-
-            @pl.when(has_up)
-            def _():
-                send_carry(n).start()
-
-        @pl.when(jnp.logical_and(n > 0, has_up))
+
+            @pl.when(jnp.logical_and(y == 2, later))
+            def _():
+                send_far(n).wait_recv()
+                gsum[...] = gin[n] + far[n]
+
+            @pl.when(jnp.logical_not(jnp.logical_and(y == 2, later)))
+            def _():
+                gsum[...] = gin[n]
+
+            tmp[1] = xin[n, 0] - apply([(block(LOW, 0), gsum)])
+            g[n, 0] = apply([(block(PIV, 0), tmp.at[1])])
+            down_rest(n, g)
+
+        @pl.when(jnp.logical_or(y == 2, jnp.logical_and(y == 1, n == 0)))
+        def _():
+            send_carry(n).start()
+
+        @pl.when(jnp.logical_and(y == 2, later))
+        def _():
+            tmp[0] = apply([(block(UP, 0), g.at[n, 1])])
+            loc[n, 0] = g[n, 0] - apply([(block(PIV, 0), tmp.at[0])])
+            send(loc.at[n, 0], zin.at[n], up_send.at[n], up_recv.at[n], (y - 1, p)).start()
+
+        @pl.when(jnp.logical_and(inner, n == 0))
+        def _():
+            form(jnp.where(y == 1, 0, 8), jnp.where(y == 1, 36, 24))
+
+        @pl.when(jnp.logical_and(later, has_up))
         def _():
             red_middle(n - 1)
 
         @pl.when(has_up)
         def _():
             send_up(n).wait_recv()
-            bacc[1] = apply([(UP, 1, zin.at[n])])
-            z[n, 1] = g[n, 1] - apply([(PIV, 1, bacc.at[1])])
+
+            @pl.when(jnp.logical_and(y == 1, later))
+            def _():
+                send_far(n).wait_recv()
+                gsum[...] = zin[n] + far[n]
+
+            @pl.when(jnp.logical_not(jnp.logical_and(y == 1, later)))
+            def _():
+                gsum[...] = zin[n]
+
+            bacc[1] = apply([(block(UP, 1), gsum)])
+            z[n, 1] = g[n, 1] - apply([(block(PIV, 1), bacc.at[1])])
             send_low(n).start()
 
         @pl.when(jnp.logical_not(has_up))
@@ -246,10 +320,19 @@
         def _():
             send_east(n, 1).start()
 
-        bacc[0] = apply([(UP, 0, z.at[n, 1])])
-        z[n, 0] = g[n, 0] - apply([(PIV, 0, bacc.at[0])])
-
-        @pl.when(has_down)
+        bacc[0] = apply([(block(UP, 0), z.at[n, 1])])
+        z[n, 0] = g[n, 0] - apply([(block(PIV, 0), bacc.at[0])])
+
+        @pl.when(jnp.logical_and(y == 3, later))
+        def _():
+            @pl.when(n == 1)
+            def _():
+                pltpu.make_async_copy(held, held, over_recv).wait()
+
+            mine[n] = apply([((held, B), z.at[n, 0])])
+            send_far(n).start()
+
+        @pl.when(jnp.logical_or(jnp.logical_or(y == 1, y == 3), jnp.logical_and(y == 2, n == 0)))
         def _():
             send_up(n).start()
 
@@ -261,14 +344,14 @@
         def _():
             send_east(n, 0).start()
 
-        @pl.when(jnp.logical_and(n > 0, jnp.logical_not(has_up)))
-        def _():
-            red_middle(n - 1)
-
-        bacc[1] = apply([(DIAG, 1, z.at[n, 1]), (LOW, 1, z.at[n, 0])], bacc[1])
-        bacc[0] = apply([(DIAG, 0, z.at[n, 0])], bacc[0])
-
-        @pl.when(n > 0)
+        @pl.when(jnp.logical_and(inner, n == 0))
+        def _():
+            form(jnp.where(y == 1, 36, 24), B)
+
+        bacc[1] = apply([(block(DIAG, 1), z.at[n, 1]), (block(LOW, 1), z.at[n, 0])], bacc[1])
+        bacc[0] = apply([(block(DIAG, 0), z.at[n, 0])], bacc[0])
+
+        @pl.when(later)
         def _():
             red_end(n - 1)
 
@@ -286,16 +369,16 @@
                 send_west(n, k).wait_recv()
 
         halo(1)
-        value = apply([(WEST, 1, hw.at[n, 1]), (EAST, 1, he.at[n, 1])], bacc[1])
+        value = apply([(block(WEST, 1), hw.at[n, 1]), (block(EAST, 1), he.at[n, 1])], bacc[1])
         xin[n + 1, 1] = combined(value, lambda i: xin[i + 1, 1])
 
         @pl.when(has_down)
         def _():
             send_low(n).wait_recv()
-            bacc[0] = apply([(LOW, 0, zlow.at[n])], bacc[0])
+            bacc[0] = apply([(block(LOW, 0), zlow.at[n])], bacc[0])
 
         halo(0)
-        value = apply([(WEST, 0, hw.at[n, 0]), (EAST, 0, he.at[n, 0])], bacc[0])
+        value = apply([(block(WEST, 0), hw.at[n, 0]), (block(EAST, 0), he.at[n, 0])], bacc[0])
         xin[n + 1, 0] = combined(value, lambda i: xin[i + 1, 0])
         return carry
 
@@ -364,11 +447,19 @@
             def _():
                 send_east(n, k).wait_send()
 
+        @pl.when(jnp.logical_and(outer, n > 0))
+        def _():
+            send_far(n).wait_send()
+
         pltpu.make_async_copy(recv1.at[n], recv1.at[n], red1_send.at[n]).wait()
         pltpu.make_async_copy(recv2.at[n], recv2.at[n], red2_send.at[n]).wait()
         return carry
 
     lax.fori_loop(0, N, drain, 0)
+
+    @pl.when(inner)
+    def _():
+        pltpu.make_async_copy(over, over, over_send).wait()
 
 
 def solution(mesh):
@@ -388,7 +479,7 @@
             out_specs=pl.BlockSpec(memory_space=pltpu.VMEM),
             scratch_shapes=[
                 pltpu.VMEM((6, 2, B, B, 128), jnp.bfloat16),
-                pltpu.VMEM((6, 2, B * B, 128), F32),
+                pltpu.VMEM((6, 2, B * PITCH, 128), F32),
                 pltpu.VMEM((N + 1, 2, B, 128), F32),
                 pair, pair, pair, pair,
                 single, single, single,
@@ -397,10 +488,14 @@
                 tile, tiles, tile, tiles, tile,
                 tile, tile,
                 pltpu.VMEM((8, 128), F32),
+                pltpu.VMEM((B * B, 128), F32), pltpu.VMEM((B * B, 128), F32),
+                single, single, pair,
+                pltpu.VMEM((2, B, 128), F32), pltpu.VMEM((B, 128), F32),
                 dma((7, 2)),
                 dma((N,)), dma((N,)), dma((N,)), dma((N,)), dma((N,)), dma((N,)),
                 dma((N, 2)), dma((N, 2)), dma((N, 2)), dma((N, 2)),
                 dma((N,)), dma((N,)), dma((N,)), dma((N,)),
+                dma, dma, dma((N,)), dma((N,)),
             ],
             compiler_params=pltpu.CompilerParams(collective_id=0, has_side_effects=True),
         )(newton_residual.reshape(2, B, 128), *arrays)

time: 112 us -> 104 us (0.929)
  Pallas kernels: 111 us -> 102 us
    pallas_call x1, Pallas kernels: 111 us -> 102 us  [per_device(): pl.pallas_call(functools.partial(kernel, lines, rows), out_shape=jax.Shap...]
where the time goes in v1:
time: 104 us
  Pallas kernels  102 us (98%)
  other arithmetic  1.42 us (1%)
    pallas_call x1, Pallas kernels, per_device(): pl.pallas_call(functools.partial(kernel, lines, rows), out_shape=jax.Shap...  102 us

profile of v1, /device:TPU:1, one launch (start us, length us, event | category | flops | bytes accessed | tf_op | source)
XLA Modules:
  0.0 103.7 jit_solution(12218400060071338098)
XLA Ops:
  0.0 102.3 %shard_map.73 = f32[2,48,128]{2,1,0:T(8,128)} custom-call(f32[2,48,128]{2,1,0:T(8,128)} %bitcast.16, bf16[2,48,48,128]{3,2,1,0:T(8,128)(2,1)} %bitcast.10, bf16[2,48,48,128]{3,2,1,0:T(8,128)(2,1)} %bitcast.11, bf16[2,48,48,128]{3,2,1,0:T(8,128)(2,1)} %bitcast.12, bf16[2,48,48,128]{3,2,1,0:T(8,128)(2,1)} %bitcast.13, bf16[2,48,48,128]{3,2,1,0:T(8,128)(2,1)} %bitcast.14, ...), custom_call_target="tpu_custom_call" | custom-call | tf_op jit(solution)/shard_map/pallas_call | solution.py:475
  102.3 1.4 %broadcast_multiply_fusion = f32[2,48,128]{2,1,0:T(8,128)} fusion(f32[2,48,128]{2,1,0:T(8,128)} %shard_map.73), kind=kLoop, calls=%fused_computation | loop fusion | flops 12288 | bytes 98304 | tf_op jit(solution)/shard_map/mul | solution.py:502

commit v2 on v1

--- a/solution.py
+++ b/solution.py
@@ -139,19 +139,37 @@
         return send(z.at[n, k], hw.at[n, k], east_send.at[n, k], east_recv.at[n, k], (y, p + 1))
 
     def send_far(n):
-        return send(mine.at[n], far.at[n], far_send.at[n], far_recv.at[n], (jnp.where(y == 0, y + 2, y - 2), p))
-
-    order = jnp.where(y == 1, 0, 1)
-    coupling = jnp.where(y == 1, LOW, UP)
-
-    def form(first, last):
+        return send(mine.at[n], far.at[n], far_send.at[n], far_recv.at[n], (y + 2, p))
+
+    def post(j):
+        rows_j = pl.ds(pl.multiple_of(j * B, 8), B)
+        send(over.at[rows_j], held.at[rows_j], over_send, over_recv, (y - 1, p)).start()
+
+    def post_all(first, last):
         def body(j, carry):
-            a = apply([((mats.at[PIV, order], PITCH), mats.at[coupling, order, pl.ds(pl.multiple_of(j * PITCH, 8), B)])])
-            col[0] = a
-            col[1] = apply([((mats.at[coupling, 1 - order], PITCH), col.at[0])])
-            over[pl.ds(pl.multiple_of(j * B, 8), B), :] = apply([((mats.at[PIV, 1 - order], PITCH), col.at[1])])
+            post(j)
+            return carry
+        lax.fori_loop(first, last, body, 0)
+
+    def form(first, last, end):
+        def body(j, carry):
             rows_j = pl.ds(pl.multiple_of(j * B, 8), B)
-            send(over.at[rows_j], held.at[rows_j], over_send, over_recv, (jnp.where(y == 1, y - 1, y + 1), p)).start()
+            col[0] = apply([(block(PIV, 0), mats.at[LOW, 0, pl.ds(pl.multiple_of(j * PITCH, 8), B)])])
+            col[1] = apply([(block(LOW, 1), col.at[0])])
+            col[2] = apply([(block(PIV, 1), col.at[1])])
+
+            @pl.when(y == 1)
+            def _():
+                over[rows_j, :] = col[2]
+
+            @pl.when(y == 3)
+            def _():
+                col[1] = apply([(block(UP, 0), col.at[2])])
+                over[rows_j, :] = -col[0] - apply([(block(PIV, 0), col.at[1])])
+
+            @pl.when(j < end)
+            def _():
+                post(j)
             return carry
         lax.fori_loop(first, last, body, 0)
 
@@ -196,8 +214,7 @@
             total = total - coef[i][None] * olds(i).reshape(6, 8, 128)
         return (total * eta[...][None]).reshape(B, 128)
 
-    inner = jnp.logical_or(y == 1, y == 2)
-    outer = jnp.logical_not(inner)
+    forms = jnp.logical_or(y == 1, y == 3)
 
     widen_all(0, 2)
     widen(LOW, 1)
@@ -209,6 +226,7 @@
 
     def stage(n, carry):
         later = n > 0
+        down_short = n > 1
 
         @pl.when(y == 0)
         def _():
@@ -219,9 +237,9 @@
         def _():
             pl.semaphore_wait(barrier, 2 * (GROUP - 1) + has_west.astype(jnp.int32) + has_east.astype(jnp.int32))
 
-        @pl.when(jnp.logical_and(y == 0, later))
-        def _():
-            @pl.when(n == 1)
+        @pl.when(jnp.logical_and(y == 0, down_short))
+        def _():
+            @pl.when(n == 2)
             def _():
                 pltpu.make_async_copy(held, held, over_recv).wait()
 
@@ -237,7 +255,7 @@
                 widen(LOW, 0)
                 widen_all(4, 12)
 
-        @pl.when(jnp.logical_and(y == 1, later))
+        @pl.when(jnp.logical_and(y == 1, down_short))
         def _():
             loc[n, 0] = apply([(block(PIV, 0), xin.at[n, 0])])
             down_rest(n, loc)
@@ -249,22 +267,27 @@
 
         @pl.when(jnp.logical_and(y == 3, later))
         def _():
+            loc[n, 0] = apply([(block(PIV, 0), xin.at[n, 0])])
+            down_rest(n, loc)
+            tmp[0] = apply([(block(UP, 0), loc.at[n, 1])])
+            mine[n] = loc[n, 0] - apply([(block(PIV, 0), tmp.at[0])])
+            send(mine.at[n], zin.at[n], up_send.at[n], up_recv.at[n], (y - 1, p)).start()
             red_middle(n - 1)
 
-        @pl.when(jnp.logical_and(y == 2, n == 0))
-        def _():
-            form(0, 8)
+        @pl.when(jnp.logical_and(y == 3, n == 0))
+        def _():
+            form(0, 22, 18)
 
         @pl.when(has_down)
         def _():
             send_carry(n).wait_recv()
 
-            @pl.when(jnp.logical_and(y == 2, later))
+            @pl.when(jnp.logical_and(y == 2, down_short))
             def _():
                 send_far(n).wait_recv()
                 gsum[...] = gin[n] + far[n]
 
-            @pl.when(jnp.logical_not(jnp.logical_and(y == 2, later)))
+            @pl.when(jnp.logical_not(jnp.logical_and(y == 2, down_short)))
             def _():
                 gsum[...] = gin[n]
 
@@ -272,21 +295,15 @@
             g[n, 0] = apply([(block(PIV, 0), tmp.at[1])])
             down_rest(n, g)
 
-        @pl.when(jnp.logical_or(y == 2, jnp.logical_and(y == 1, n == 0)))
+        @pl.when(jnp.logical_or(y == 2, jnp.logical_and(y == 1, jnp.logical_not(down_short))))
         def _():
             send_carry(n).start()
 
-        @pl.when(jnp.logical_and(y == 2, later))
-        def _():
-            tmp[0] = apply([(block(UP, 0), g.at[n, 1])])
-            loc[n, 0] = g[n, 0] - apply([(block(PIV, 0), tmp.at[0])])
-            send(loc.at[n, 0], zin.at[n], up_send.at[n], up_recv.at[n], (y - 1, p)).start()
-
-        @pl.when(jnp.logical_and(inner, n == 0))
-        def _():
-            form(jnp.where(y == 1, 0, 8), jnp.where(y == 1, 36, 24))
-
-        @pl.when(jnp.logical_and(later, has_up))
+        @pl.when(jnp.logical_and(y == 1, n == 0))
+        def _():
+            form(0, 36, 16)
+
+        @pl.when(jnp.logical_and(later, y < 2))
         def _():
             red_middle(n - 1)
 
@@ -294,12 +311,15 @@
         def _():
             send_up(n).wait_recv()
 
-            @pl.when(jnp.logical_and(y == 1, later))
-            def _():
-                send_far(n).wait_recv()
-                gsum[...] = zin[n] + far[n]
-
-            @pl.when(jnp.logical_not(jnp.logical_and(y == 1, later)))
+            @pl.when(jnp.logical_and(y == 2, later))
+            def _():
+                @pl.when(n == 1)
+                def _():
+                    pltpu.make_async_copy(held, held, over_recv).wait()
+
+                gsum[...] = apply([((held, B), g.at[n, 1])], zin[n])
+
+            @pl.when(jnp.logical_not(jnp.logical_and(y == 2, later)))
             def _():
                 gsum[...] = zin[n]
 
@@ -323,16 +343,7 @@
         bacc[0] = apply([(block(UP, 0), z.at[n, 1])])
         z[n, 0] = g[n, 0] - apply([(block(PIV, 0), bacc.at[0])])
 
-        @pl.when(jnp.logical_and(y == 3, later))
-        def _():
-            @pl.when(n == 1)
-            def _():
-                pltpu.make_async_copy(held, held, over_recv).wait()
-
-            mine[n] = apply([((held, B), z.at[n, 0])])
-            send_far(n).start()
-
-        @pl.when(jnp.logical_or(jnp.logical_or(y == 1, y == 3), jnp.logical_and(y == 2, n == 0)))
+        @pl.when(jnp.logical_or(jnp.logical_or(y == 1, y == 2), jnp.logical_and(y == 3, n == 0)))
         def _():
             send_up(n).start()
 
@@ -344,9 +355,14 @@
         def _():
             send_east(n, 0).start()
 
-        @pl.when(jnp.logical_and(inner, n == 0))
-        def _():
-            form(jnp.where(y == 1, 36, 24), B)
+        @pl.when(jnp.logical_and(y == 2, later))
+        def _():
+            red_middle(n - 1)
+
+        @pl.when(jnp.logical_and(forms, n == 0))
+        def _():
+            post_all(jnp.where(y == 1, 16, 18), jnp.where(y == 1, 36, 22))
+            form(jnp.where(y == 1, 36, 22), B, B)
 
         bacc[1] = apply([(block(DIAG, 1), z.at[n, 1]), (block(LOW, 1), z.at[n, 0])], bacc[1])
         bacc[0] = apply([(block(DIAG, 0), z.at[n, 0])], bacc[0])
@@ -447,7 +463,7 @@
             def _():
                 send_east(n, k).wait_send()
 
-        @pl.when(jnp.logical_and(outer, n > 0))
+        @pl.when(jnp.logical_and(y == 0, n > 1))
         def _():
             send_far(n).wait_send()
 
@@ -457,7 +473,7 @@
 
     lax.fori_loop(0, N, drain, 0)
 
-    @pl.when(inner)
+    @pl.when(forms)
     def _():
         pltpu.make_async_copy(over, over, over_send).wait()
 
@@ -490,7 +506,7 @@
                 pltpu.VMEM((8, 128), F32),
                 pltpu.VMEM((B * B, 128), F32), pltpu.VMEM((B * B, 128), F32),
                 single, single, pair,
-                pltpu.VMEM((2, B, 128), F32), pltpu.VMEM((B, 128), F32),
+                pltpu.VMEM((3, B, 128), F32), pltpu.VMEM((B, 128), F32),
                 dma((7, 2)),
                 dma((N,)), dma((N,)), dma((N,)), dma((N,)), dma((N,)), dma((N,)),
                 dma((N, 2)), dma((N, 2)), dma((N, 2)), dma((N, 2)),

time: 104 us -> 92 us (0.88)
  Pallas kernels: 102 us -> 90.4 us
    pallas_call x1, Pallas kernels: 102 us -> 90.4 us  [per_device(): pl.pallas_call(functools.partial(kernel, lines, rows), out_shape=jax.Shap...]
where the time goes in v2:
time: 92 us; the launch traced here: 91.8 us
  Pallas kernels  90.4 us (98%)
  other arithmetic  1.42 us (2%)
    pallas_call x1, Pallas kernels, per_device(): pl.pallas_call(functools.partial(kernel, lines, rows), out_shape=jax.Shap...  90.4 us

profile of v2, /device:TPU:1, one launch (start us, length us, event | category | flops | bytes accessed | tf_op | source)
XLA Modules:
  0.0 91.8 jit_solution(15931560192553355720)
XLA Ops:
  0.0 90.4 %shard_map.73 = f32[2,48,128]{2,1,0:T(8,128)} custom-call(f32[2,48,128]{2,1,0:T(8,128)} %bitcast.16, bf16[2,48,48,128]{3,2,1,0:T(8,128)(2,1)} %bitcast.10, bf16[2,48,48,128]{3,2,1,0:T(8,128)(2,1)} %bitcast.11, bf16[2,48,48,128]{3,2,1,0:T(8,128)(2,1)} %bitcast.12, bf16[2,48,48,128]{3,2,1,0:T(8,128)(2,1)} %bitcast.13, bf16[2,48,48,128]{3,2,1,0:T(8,128)(2,1)} %bitcast.14, ...), custom_call_target="tpu_custom_call" | custom-call | tf_op jit(solution)/shard_map/pallas_call | solution.py:491
  90.4 1.4 %broadcast_multiply_fusion = f32[2,48,128]{2,1,0:T(8,128)} fusion(f32[2,48,128]{2,1,0:T(8,128)} %shard_map.73), kind=kLoop, calls=%fused_computation | loop fusion | flops 12288 | bytes 98304 | tf_op jit(solution)/shard_map/mul | solution.py:518

commit v3 on v2

--- a/solution.py
+++ b/solution.py
@@ -265,6 +265,10 @@
         def _():
             red_start(n - 1)
 
+        @pl.when(jnp.logical_and(y == 1, n == 1))
+        def _():
+            post_all(32, B)
+
         @pl.when(jnp.logical_and(y == 3, later))
         def _():
             loc[n, 0] = apply([(block(PIV, 0), xin.at[n, 0])])
@@ -272,11 +276,14 @@
             tmp[0] = apply([(block(UP, 0), loc.at[n, 1])])
             mine[n] = loc[n, 0] - apply([(block(PIV, 0), tmp.at[0])])
             send(mine.at[n], zin.at[n], up_send.at[n], up_recv.at[n], (y - 1, p)).start()
+
+        @pl.when(jnp.logical_and(y == 3, n < 2))
+        def _():
+            form(jnp.where(later, 38, 0), jnp.where(later, B, 22), jnp.where(later, B, 18))
+
+        @pl.when(jnp.logical_and(y == 3, later))
+        def _():
             red_middle(n - 1)
-
-        @pl.when(jnp.logical_and(y == 3, n == 0))
-        def _():
-            form(0, 22, 18)
 
         @pl.when(has_down)
         def _():
@@ -301,7 +308,7 @@
 
         @pl.when(jnp.logical_and(y == 1, n == 0))
         def _():
-            form(0, 36, 16)
+            form(0, 36, 20)
 
         @pl.when(jnp.logical_and(later, y < 2))
         def _():
@@ -361,8 +368,9 @@
 
         @pl.when(jnp.logical_and(forms, n == 0))
         def _():
-            post_all(jnp.where(y == 1, 16, 18), jnp.where(y == 1, 36, 22))
-            form(jnp.where(y == 1, 36, 22), B, B)
+            post_all(jnp.where(y == 1, 20, 18), jnp.where(y == 1, 32, 22))
+            form(jnp.where(y == 1, 36, 22), jnp.where(y == 1, B, 38), jnp.where(y == 1, 0, B))
+
 
         bacc[1] = apply([(block(DIAG, 1), z.at[n, 1]), (block(LOW, 1), z.at[n, 0])], bacc[1])
         bacc[0] = apply([(block(DIAG, 0), z.at[n, 0])], bacc[0])
@@ -400,44 +408,51 @@
 
     lax.fori_loop(0, N, stage, 0)
     red_start(N - 1)
+
+    zero = jnp.zeros((8, 128), F32)
+
+    def entry(m, i):
+        return res[m, pl.ds(i, 8, stride=0), :]
+
+    size = [jnp.sqrt(gam[i]) for i in range(N - 1)]
+    turns = []
+    upper = {}
+    target = [size[0]] + [zero] * N
+
+    def column(m, below):
+        value = [entry(m, i) / (size[i] * size[m]) for i in range(m + 1)] + [below]
+        for k, (cosine, sine) in enumerate(turns):
+            value[k], value[k + 1] = (
+                cosine * value[k] + sine * value[k + 1],
+                cosine * value[k + 1] - sine * value[k],
+            )
+        radius = jnp.sqrt(value[m] * value[m] + below * below)
+        turns.append((value[m] / radius, below / radius))
+        cosine, sine = turns[m]
+        value[m] = cosine * value[m] + sine * below
+        target[m], target[m + 1] = (
+            cosine * target[m] + sine * target[m + 1],
+            cosine * target[m + 1] - sine * target[m],
+        )
+        for i in range(m + 1):
+            upper[i, m] = value[i]
+
+    for m in range(N - 2):
+        column(m, size[m + 1] * jnp.sqrt(entry(m, 5)) / size[m])
     red_middle(N - 1)
     red_end(N - 1)
-
-    size = [jnp.sqrt(gam[i]) for i in range(N)]
-    zero = jnp.zeros((8, 128), F32)
-
-    def entry(m, i):
-        return res[m, pl.ds(i, 8, stride=0), :]
-
-    hess = [[zero] * N for _ in range(N + 1)]
-    for m in range(N):
-        for i in range(m + 1):
-            hess[i][m] = entry(m, i) / (size[i] * size[m])
-        if m < N - 1:
-            hess[m + 1][m] = size[m + 1] * jnp.sqrt(entry(m, 5)) / size[m]
-        else:
-            rest = entry(m, 5)
-            for i in range(N):
-                rest = rest - entry(m, i) * entry(m, i) / gam[i]
-            hess[N][m] = jnp.sqrt(jnp.maximum(rest, 0.0)) / size[m]
-    target = [size[0]] + [zero] * N
-    for j in range(N):
-        one, two = hess[j][j], hess[j + 1][j]
-        radius = jnp.sqrt(one * one + two * two)
-        cosine, sine = one / radius, two / radius
-        top = [cosine * hess[j][i] + sine * hess[j + 1][i] for i in range(N)]
-        hess[j + 1] = [cosine * hess[j + 1][i] - sine * hess[j][i] for i in range(N)]
-        hess[j] = top
-        target[j], target[j + 1] = (
-            cosine * target[j] + sine * target[j + 1],
-            cosine * target[j + 1] - sine * target[j],
-        )
+    size.append(jnp.sqrt(gam[N - 1]))
+    column(N - 2, size[N - 1] * jnp.sqrt(entry(N - 2, 5)) / size[N - 2])
+    rest = entry(N - 1, 5)
+    for i in range(N):
+        rest = rest - entry(N - 1, i) * entry(N - 1, i) / gam[i]
+    column(N - 1, jnp.sqrt(jnp.maximum(rest, 0.0)) / size[N - 1])
     answer = [None] * N
     for i in reversed(range(N)):
         value = target[i]
         for k in range(i + 1, N):
-            value = value - hess[i][k] * answer[k]
-        answer[i] = value / hess[i][i]
+            value = value - upper[i, k] * answer[k]
+        answer[i] = value / upper[i, i]
     for k in range(2):
         total = jnp.zeros((6, 8, 128), F32)
         for i in range(N):

time: 92 us -> 90.8 us (0.987)
  Pallas kernels: 90.4 us -> 89.3 us
    pallas_call x1, Pallas kernels: 90.4 us -> 89.3 us  [per_device(): pl.pallas_call(functools.partial(kernel, lines, rows), out_shape=jax.Shap...]
where the time goes in v3:
time: 90.8 us; the launch traced here: 90.7 us
  Pallas kernels  89.3 us (98%)
  other arithmetic  1.42 us (2%)
    pallas_call x1, Pallas kernels, per_device(): pl.pallas_call(functools.partial(kernel, lines, rows), out_shape=jax.Shap...  89.3 us

profile of v3, /device:TPU:1, one launch (start us, length us, event | category | flops | bytes accessed | tf_op | source)
XLA Modules:
  0.0 90.7 jit_solution(7675599394292951544)
XLA Ops:
  0.0 89.3 %shard_map.73 = f32[2,48,128]{2,1,0:T(8,128)} custom-call(f32[2,48,128]{2,1,0:T(8,128)} %bitcast.16, bf16[2,48,48,128]{3,2,1,0:T(8,128)(2,1)} %bitcast.10, bf16[2,48,48,128]{3,2,1,0:T(8,128)(2,1)} %bitcast.11, bf16[2,48,48,128]{3,2,1,0:T(8,128)(2,1)} %bitcast.12, bf16[2,48,48,128]{3,2,1,0:T(8,128)(2,1)} %bitcast.13, bf16[2,48,48,128]{3,2,1,0:T(8,128)(2,1)} %bitcast.14, ...), custom_call_target="tpu_custom_call" | custom-call | tf_op jit(solution)/shard_map/pallas_call | solution.py:506
  89.3 1.4 %broadcast_multiply_fusion = f32[2,48,128]{2,1,0:T(8,128)} fusion(f32[2,48,128]{2,1,0:T(8,128)} %shard_map.73), kind=kLoop, calls=%fused_computation | loop fusion | flops 12288 | bytes 98304 | tf_op jit(solution)/shard_map/mul | solution.py:533
